TPU v7x, 32 devices: a whole 2x2x4 slice. The times are simulated.
32 devices in a mesh: row: 4 (over y, core), col: 8 (over z, x).
Axes of the slice: x: 2, y: 2, z: 4, core: 2. Of those that a mesh axis runs over, the one named last changes fastest.
Arguments:
- ainv_top: float32 [4096, 4096], P('row', 'col'), may hold values from -0.25 to 0.25
- par_struct: int32 [8, 16], replicated, may hold values from 0 to 31, as said below
- par_panel: float32 [8, 16, 128, 128], P('col', 'row'), may hold values from -6 to 6
- par_linv: float32 [8, 128, 128], P('col', 'row'), may hold values from -0.0625 to 0.0625
- par_dinv: float32 [8, 128, 128], P('col', 'row'), may hold values from -192 to 192
- kid_panel: float32 [16, 16, 128, 128], P('col', 'row'), may hold values from -6 to 6
- kid_upper: float32 [16, 128, 128], P('col', 'row'), may hold values from -6 to 6
- kid_linv: float32 [16, 128, 128], P('col', 'row'), may hold values from -0.0625 to 0.0625
- kid_dinv: float32 [16, 128, 128], P('col', 'row'), may hold values from -192 to 192
Outputs:
- par_offdiag: float32 [8, 16, 128, 128], P('col', 'row')
- par_diag: float32 [8, 128, 128], P('col', 'row')
- kid_offdiag: float32 [16, 16, 128, 128], P('col', 'row')
- kid_parent: float32 [16, 128, 128], P('col', 'row')
- kid_diag: float32 [16, 128, 128], P('col', 'row')
Inputs may be any that keep to these rules, and one draw needn't show every extreme that they name: `par_struct`: in every row, entries 2j and 2j + 1 are two different ancestors among j * 4 to (j + 1) * 4 - 1.
All inputs are finite; a program needn't handle non-finite values.
Results may differ from a plain program's by a relative error of at most 0.00014.
Values sent between devices are 32-bit elements; how exact they have to be, the bound alone decides.
No kernel may reach another device: no remote copies, remote signals or barrier semaphores. Data moves between devices by JAX's collectives and lax.ppermute only.
A program may use at most 128 MiB of HBM per device.

v0:
```python
import jax
import jax.numpy as jnp
from jax import lax
from jax.sharding import PartitionSpec as P

highest = lax.Precision.HIGHEST


def spread(array, axis, root):
    mine = lax.axis_index(axis) == root
    return lax.psum(jnp.where(mine, array, jnp.zeros_like(array)), axis)


def on_device(
    ainv_top, par_struct, par_panel, par_linv, par_dinv, kid_panel, kid_upper, kid_linv, kid_dinv
):
    grid_rows = lax.axis_size("row")
    grid_cols = lax.axis_size("col")
    my_row = lax.axis_index("row")
    my_col = lax.axis_index("col")
    tile_width = par_panel.shape[-1]
    band_rows = tile_width // grid_rows
    parents = par_panel.shape[0]
    slot_share = par_panel.shape[1]
    children = kid_panel.shape[0]
    brood = children // parents
    slots_all = par_struct.shape[1]
    pair_width = slots_all // grid_cols
    tile_rows = ainv_top.shape[0] // tile_width
    tile_cols = ainv_top.shape[1] // tile_width
    local_tiles = ainv_top.reshape(tile_rows, tile_width, tile_cols, tile_width)
    row_base = my_row * tile_rows
    col_base = my_col * tile_cols
    band_start = my_row * band_rows
    par_linv_full, par_dinv_full = (
        lax.all_gather(par_linv, "row", axis=1, tiled=True),
        lax.all_gather(par_dinv, "row", axis=1, tiled=True),
    )
    par_hat = jnp.einsum("psij,pjk->psik", par_panel, par_linv_full, precision=highest)
    owner_rows = lax.dynamic_slice_in_dim(par_struct, my_row * slot_share, slot_share, 1) - row_base
    owner_cols = lax.dynamic_slice_in_dim(par_struct, my_col * pair_width, pair_width, 1) - col_base
    root_row = my_col * pair_width // slot_share
    within = my_col * pair_width - root_row * slot_share
    every_hat = lax.all_gather(par_hat, "col", axis=0, tiled=True)
    picked = lax.dynamic_slice_in_dim(every_hat, within, pair_width, 1)
    picked = spread(picked, "row", root_row)
    rows_here = owner_rows
    cols_here = owner_cols
    picks_here = picked
    tiles_here = local_tiles[rows_here[:, :, None], :, cols_here[:, None, :], :]
    par_prod = lax.psum_scatter(
        jnp.einsum("pjkab,pkbc->pjac", tiles_here, picks_here, precision=highest),
        "col",
        scatter_dimension=0,
        tiled=True,
    )
    par_off = -par_prod
    pivot_term = jnp.einsum(
        "pji,pjk,pkl->pil", par_linv_full, par_dinv_full, par_linv_full, precision=highest
    )
    diag_part = -jnp.einsum("psji,psjk->pik", par_hat, par_off, precision=highest)
    par_diag_full = pivot_term + lax.psum(diag_part, "row")
    par_diag_band = lax.dynamic_slice_in_dim(par_diag_full, band_start, band_rows, 1)
    kid_upper_full, kid_linv_full, kid_dinv_full = (
        lax.all_gather(kid_upper, "row", axis=1, tiled=True),
        lax.all_gather(kid_linv, "row", axis=1, tiled=True),
        lax.all_gather(kid_dinv, "row", axis=1, tiled=True),
    )
    kid_hat = jnp.einsum("csij,cjk->csik", kid_panel, kid_linv_full, precision=highest)
    kid_uphat = jnp.einsum("cij,cjk->cik", kid_upper_full, kid_linv_full, precision=highest)
    kid_rows = jnp.repeat(owner_rows, brood, axis=0)
    kid_cols = jnp.repeat(owner_cols, brood, axis=0)
    every_kid = lax.all_gather(kid_hat, "col", axis=0, tiled=True)
    kid_picked = lax.dynamic_slice_in_dim(every_kid, within, pair_width, 1)
    kid_picked = spread(kid_picked, "row", root_row)
    rows_here = kid_rows
    cols_here = kid_cols
    picks_here = kid_picked
    tiles_here = local_tiles[rows_here[:, :, None], :, cols_here[:, None, :], :]
    kid_prod = lax.psum_scatter(
        jnp.einsum("pjkab,pkbc->pjac", tiles_here, picks_here, precision=highest),
        "col",
        scatter_dimension=0,
        tiled=True,
    )
    uphat_grouped = kid_uphat.reshape(parents, brood, tile_width, tile_width)
    kid_off = -(
        kid_prod.reshape(parents, brood, slot_share, tile_width, tile_width)
        + jnp.einsum("pjab,pibc->pijac", par_off, uphat_grouped, precision=highest)
    )
    kid_off = kid_off.reshape(children, slot_share, tile_width, tile_width)
    linv_band = lax.dynamic_slice_in_dim(kid_linv_full, band_start, band_rows, 2)
    kid_pivot_band = jnp.einsum(
        "cji,cjk,ckl->cil", linv_band, kid_dinv_full, kid_linv_full, precision=highest
    )
    parent_part = jnp.einsum(
        "pjba,pijbc->piac",
        par_off,
        kid_hat.reshape(parents, brood, slot_share, tile_width, tile_width),
        precision=highest,
    ).reshape(children, tile_width, tile_width)
    hat_part = -jnp.einsum("csji,csjk->cik", kid_hat, kid_off, precision=highest)
    diag_times = jnp.einsum(
        "pab,pibc->piac", par_diag_full, uphat_grouped, precision=highest
    ).reshape(children, tile_width, tile_width)
    uphat_band = lax.dynamic_slice_in_dim(kid_uphat, band_start, band_rows, 2)
    parent_sum = lax.psum(parent_part, "row")
    kid_par_full = -(parent_sum + diag_times)
    diag_sum = lax.psum_scatter(hat_part, "row", scatter_dimension=1, tiled=True)
    kid_diag_band = (
        kid_pivot_band
        + diag_sum
        - jnp.einsum("cji,cjk->cik", uphat_band, kid_par_full, precision=highest)
    )
    kid_par_band = lax.dynamic_slice_in_dim(kid_par_full, band_start, band_rows, 1)
    return (par_off, par_diag_band, kid_off, kid_par_band, kid_diag_band)


def solution(mesh):
    placed = (
        P("row", "col"),
        P(),
        P("col", "row", None, None),
        P("col", "row", None),
        P("col", "row", None),
        P("col", "row", None, None),
        P("col", "row", None),
        P("col", "row", None),
        P("col", "row", None),
    )
    return jax.shard_map(
        on_device,
        mesh=mesh,
        in_specs=placed,
        out_specs=(
            P("col", "row", None, None),
            P("col", "row", None),
            P("col", "row", None, None),
            P("col", "row", None),
            P("col", "row", None),
        ),
        check_vma=False,
    )
```

profile of v0, /device:TPU:0, one launch (start us, length us, event | category | flops | bytes accessed | tf_op | source)
XLA Modules:
  0.0 442.1 jit_solution(8733068069592860143)
XLA Ops:
  7.2 6.6 %all_gather.21 = f32[1,128,128]{2,1,0:T(8,128)S(1)} all-gather(f32[1,32,128]{2,1,0:T(8,128)} %param.12), channel_id=1, replica_groups=mesh['row'=4,'col'=8] {'row'}, dimensions={1}, use_global_device_ids=true | all-gather | bytes 81920 | tf_op jit(solution)/shard_map/all_gather | solution.py:36
  14.4 2.0 fusion.14
  16.6 51.1 %all-gather.6.cloned.1.call-done = f32[32,128,128]{2,1,0:T(8,128)} async-done(((f32[4,128,128]{2,1,0:T(8,128)}), f32[32,128,128]{2,1,0:T(8,128)}) %all-gather.6.cloned.1.call-update) | async-done | bytes 2097168 | tf_op jit(solution)/shard_map/all_gather | solution.py:44
  67.7 2.3 dynamic-slice_select_fusion.1
  70.1 5.6 %all_gather.24 = f32[2,128,128]{2,1,0:T(8,128)S(1)} all-gather(f32[2,32,128]{2,1,0:T(8,128)} %param.16), channel_id=1, replica_groups=mesh['row'=4,'col'=8] {'row'}, dimensions={1}, use_global_device_ids=true | all-gather | bytes 163840 | tf_op jit(solution)/shard_map/all_gather | solution.py:66
  75.7 1.4 fusion.17
  77.2 1.7 reshape.154
  78.9 1.9 copy.51
  81.2 2.9 gather_fusion
  84.0 20.7 %all-reduce.4.cloned.1.call-done = f32[8,2,128,128]{3,2,1,0:T(8,128)} async-done(((f32[8,2,128,128]{3,2,1,0:T(8,128)}), f32[8,2,128,128]{3,2,1,0:T(8,128)}) %all-reduce.4.cloned.1.call-update) | async-done | bytes 1048592 | tf_op jit(solution)/shard_map/psum | solution.py:11
  104.7 7.5 %convolution_bitcast_fusion.1 = f32[8,4,128,128]{3,2,1,0:T(8,128)} fusion(f32[8,4,2,128,128]{4,3,2,1,0:T(8,128)} %bitcast.127, f32[8,2,128,128]{3,2,1,0:T(8,128)} %all-reduce.4.cloned.1.call-done), kind=kOutput, calls=%fused_computation.5 | convolution fusion | flops 1610612736 | bytes 7340032 | tf_op jit(solution)/shard_map/pjkab,pkbc->pjac/dot_general | solution.py:52
  112.3 69.1 %all-gather.4.cloned.1.call-done = f32[16,4,128,128]{3,2,1,0:T(8,128)} async-done(((f32[2,4,128,128]{3,2,1,0:T(8,128)}), f32[16,4,128,128]{3,2,1,0:T(8,128)}) %all-gather.4.cloned.1.call-update) | async-done | bytes 4194320 | tf_op jit(solution)/shard_map/all_gather | solution.py:73
  181.5 3.2 dynamic-slice_select_fusion
  184.7 66.5 %reduce-scatter.4.cloned.1.call-done = f32[1,4,128,128]{3,2,1,0:T(8,128)} async-done(((f32[8,4,128,128]{3,2,1,0:T(8,128)}), f32[1,4,128,128]{3,2,1,0:T(8,128)}) %reduce-scatter.4.cloned.1.call-update) | async-done | bytes 262160 | tf_op jit(solution)/shard_map/reduce_scatter | solution.py:51
  251.2 1.0 neg.18
  252.2 2.3 fusion.8
  254.5 1.7 convolution_bitcast_fusion.4
  257.2 0.8 copy.54
  258.0 0.7 broadcast_or_fusion
  258.7 0.9 reshape.135
  259.6 4.5 %gather_fusion.1 = f32[128,128,128]{2,1,0:T(8,128)} fusion(f32[8,128,4,128]{3,1,2,0:T(8,128)S(1)} %copy.51, s32[128]{0:T(128)S(1)} %reshape.135), kind=kCustom, calls=%fused_computation.1 | custom fusion | bytes 16778240 | tf_op jit(solution)/shard_map/gather | solution.py:79
  264.0 46.2 %all-reduce.6.cloned.1.call-done = (f32[1,128,128]{2,1,0:T(8,128)}, f32[16,2,128,128]{3,2,1,0:T(8,128)}, f32[2,128,128]{1,2,0:T(8,128)}) async-done(((f32[1,128,128]{2,1,0:T(8,128)}, f32[16,2,128,128]{3,2,1,0:T(8,128)}, f32[2,128,128]{1,2,0:T(8,128)}), (f32[1,128,128]{2,1,0:T(8,128)}, f32[16,2,128,128]{3,2,1,0:T(8,128)}, f32[2,128,128]{1,2,0:T(8,128)})) %all-reduce.6.cloned.1.call-update) | async-done | bytes 2293776 | tf_op jit(solution)/shard_map/psum | solution.py:62
  310.3 12.1 %convolution_bitcast_fusion = f32[16,4,128,128]{3,2,1,0:T(8,128)} fusion(f32[16,4,2,128,128]{4,3,2,1,0:T(8,128)} %bitcast.126, f32[16,2,128,128]{3,2,1,0:T(8,128)} %get-tuple-element.26), kind=kOutput, calls=%fused_computation.2 | convolution fusion | flops 3221225472 | bytes 14680064 | tf_op jit(solution)/shard_map/pjkab,pkbc->pjac/dot_general | solution.py:81
  323.0 5.2 %all_gather.23 = f32[1,128,128]{2,1,0:T(8,128)S(1)} all-gather(f32[1,32,128]{2,1,0:T(8,128)S(1)} %copy-done.11), channel_id=1, replica_groups=mesh['row'=4,'col'=8] {'row'}, dimensions={1}, use_global_device_ids=true | all-gather | bytes 81920 | tf_op jit(solution)/shard_map/all_gather | solution.py:37
  328.3 5.4 %all_gather.26 = f32[2,128,128]{2,1,0:T(8,128)S(1)} all-gather(f32[2,32,128]{2,1,0:T(8,128)S(1)} %copy-done.9), channel_id=1, replica_groups=mesh['row'=4,'col'=8] {'row'}, dimensions={1}, use_global_device_ids=true | all-gather | bytes 163840 | tf_op jit(solution)/shard_map/all_gather | solution.py:65
  333.7 5.4 %all_gather.27 = f32[2,128,128]{2,1,0:T(8,128)S(1)} all-gather(f32[2,32,128]{2,1,0:T(8,128)S(1)} %copy-done.10), channel_id=1, replica_groups=mesh['row'=4,'col'=8] {'row'}, dimensions={1}, use_global_device_ids=true | all-gather | bytes 163840 | tf_op jit(solution)/shard_map/all_gather | solution.py:67
  340.5 70.0 %reduce-scatter.6.cloned.1.call-done = f32[2,4,128,128]{3,2,1,0:T(8,128)} async-done(((f32[16,4,128,128]{3,2,1,0:T(8,128)}), f32[2,4,128,128]{3,2,1,0:T(8,128)}) %reduce-scatter.6.cloned.1.call-update) | async-done | bytes 524304 | tf_op jit(solution)/shard_map/reduce_scatter | solution.py:80
  410.5 1.6 fusion.3
  412.2 1.7 fusion.4
  415.6 17.8 %reduce-scatter.8.cloned.1.call-done = f32[2,32,128]{2,1,0:T(8,128)} async-done(((f32[2,128,128]{2,1,0:T(8,128)}), f32[2,32,128]{2,1,0:T(8,128)}) %reduce-scatter.8.cloned.1.call-update) | async-done | bytes 32784 | tf_op jit(solution)/shard_map/reduce_scatter | solution.py:109
  433.4 1.0 convolution_add_fusion
  434.3 0.9 convolution_subtract_fusion
  (58 shorter events, 6.1 us)
Async XLA Ops:
  7.2 68.5 %copy-start = (f32[2,4,128,128]{3,2,1,0:T(8,128)S(1)}, f32[2,4,128,128]{3,2,1,0:T(8,128)}, u32[]{:S(2)}) copy-start(f32[2,4,128,128]{3,2,1,0:T(8,128)} %param.14) | copy-start | bytes 1572868
  7.2 70.0 %copy-start.3 = (f32[1024,512]{1,0:T(8,128)S(1)}, f32[1024,512]{1,0:T(8,128)}, u32[]{:S(2)}) copy-start(f32[1024,512]{1,0:T(8,128)} %param.9) | copy-start | bytes 6291460
  7.2 60.5 %all-gather.6.cloned.1.call-start = ((), (), s32[]{:S(2)}) async-start(), calls=%async_computation.8 | async-start | bytes 2359296 | tf_op jit(solution)/shard_map/all_gather | solution.py:44
  13.8 0.6 copy-start.5
  16.5 88.2 %all-reduce.4.cloned.1.call-start = ((), (), s32[]{:S(2)}) async-start(), calls=%async_computation.3 | async-start | bytes 2097152 | tf_op jit(solution)/shard_map/psum | solution.py:11
  70.0 111.5 %all-gather.4.cloned.1.call-start = ((), (), s32[]{:S(2)}) async-start(), calls=%async_computation.5 | async-start | bytes 4718592 | tf_op jit(solution)/shard_map/all_gather | solution.py:73
  77.1 174.1 %reduce-scatter.4.cloned.1.call-start = ((), (), s32[]{:S(2)}) async-start(), calls=%async_computation.4 | async-start | bytes 2359296 | tf_op jit(solution)/shard_map/reduce_scatter | solution.py:51
  77.2 3.6 copy-start.12
  112.3 142.2 %copy-start.1 = (f32[2,4,128,128]{3,2,1,0:T(8,128)S(1)}, f32[2,4,128,128]{3,2,1,0:T(8,128)}, u32[]{:S(2)}) copy-start(f32[2,4,128,128]{3,2,1,0:T(8,128)} %fusion.17) | copy-start | bytes 1572868
  112.3 198.0 %all-reduce.6.cloned.1.call-start = ((), (), s32[]{:S(2)}) async-start(), calls=%async_computation.9 | async-start | bytes 4587520 | tf_op jit(solution)/shard_map/psum | solution.py:62
  252.2 158.4 %copy-start.2 = (f32[1,4,128,128]{3,2,1,0:T(8,128)}, f32[1,4,128,128]{3,2,1,0:T(8,128)S(1)}, u32[]{:S(2)}) copy-start(f32[1,4,128,128]{3,2,1,0:T(8,128)S(1)} %neg.18) | copy-start | bytes 786436
  256.1 154.4 %reduce-scatter.6.cloned.1.call-start = ((), (), s32[]{:S(2)}) async-start(), calls=%async_computation.6 | async-start | bytes 4718592 | tf_op jit(solution)/shard_map/reduce_scatter | solution.py:80
  322.3 0.7 copy-start.11
  322.3 5.9 %copy-start.9 = (f32[2,32,128]{2,1,0:T(8,128)S(1)}, f32[2,32,128]{2,1,0:T(8,128)}, u32[]{:S(2)}) copy-start(f32[2,32,128]{2,1,0:T(8,128)} %param.15) | copy-start | bytes 98308
  322.3 11.4 %copy-start.10 = (f32[2,32,128]{2,1,0:T(8,128)S(1)}, f32[2,32,128]{2,1,0:T(8,128)}, u32[]{:S(2)}) copy-start(f32[2,32,128]{2,1,0:T(8,128)} %param.17) | copy-start | bytes 98308
  322.3 17.2 %copy-start.6 = (f32[1,128,128]{2,1,0:T(8,128)S(1)}, f32[1,128,128]{2,1,0:T(8,128)}, u32[]{:S(2)}) copy-start(f32[1,128,128]{2,1,0:T(8,128)} %copy-done.5) | copy-start | bytes 196612
  322.4 17.9 %copy-start.8 = (f32[1,128,128]{2,1,0:T(8,128)S(1)}, f32[1,128,128]{2,1,0:T(8,128)}, u32[]{:S(2)}) copy-start(f32[1,128,128]{2,1,0:T(8,128)} %get-tuple-element.25) | copy-start | bytes 196612
  322.4 91.5 %copy-start.7 = (f32[2,128,128]{1,2,0:T(8,128)S(1)}, f32[2,128,128]{1,2,0:T(8,128)}, u32[]{:S(2)}) copy-start(f32[2,128,128]{1,2,0:T(8,128)} %get-tuple-element.27) | copy-start | bytes 393220
  322.4 111.0 %reduce-scatter.8.cloned.1.call-start = ((), (), s32[]{:S(2)}) async-start(), calls=%async_computation.7 | async-start | bytes 163840 | tf_op jit(solution)/shard_map/reduce_scatter | solution.py:109
  412.2 23.1 %copy-start.4 = (f32[2,4,128,128]{3,2,1,0:T(8,128)}, f32[2,4,128,128]{3,2,1,0:T(8,128)S(1)}, u32[]{:S(2)}) copy-start(f32[2,4,128,128]{3,2,1,0:T(8,128)S(1)} %fusion.3) | copy-start | bytes 1572868
Sparse Core Ops, SparseCore 0:
  16.6 50.9 all-gather.5
  70.1 34.5 all-reduce.3
  107.7 73.7 all-gather.3
  185.3 65.8 reduce-scatter.3
  256.3 53.9 all-reduce.5
  322.5 87.9 reduce-scatter.5
  414.0 19.3 reduce-scatter.7
where the time goes:
time: 443 us; the launch traced here: 442 us
  waiting for transfers between devices  342 us (77%)
  matrix products  33.7 us (8%)
  blocking collectives  28.3 us (6%)
  local copies, waits for them, and re-layouts  15.7 us (4%)
  between operations  14.4 us (3%)
  other arithmetic  8.02 us (2%)
    reduce_scatter x2, waiting for transfers between devices, on_device(): lax.psum_scatter(jnp.einsum('pjkab,pkbc->pjac', tiles_here, picks_here, p...  137 us
    all_gather x1, waiting for transfers between devices, on_device(): every_kid = lax.all_gather(kid_hat, 'col', axis=0, tiled=True)  69.1 us
    all_gather x1, waiting for transfers between devices, on_device(): every_hat = lax.all_gather(par_hat, 'col', axis=0, tiled=True)  51.1 us
    psum x1, waiting for transfers between devices, on_device(): par_diag_full = pivot_term + lax.psum(diag_part, 'row')  46.2 us
    psum x1, waiting for transfers between devices, spread(): return lax.psum(jnp.where(mine, array, jnp.zeros_like(array)), axis)  20.7 us
    dot_general x2, matrix products, on_device(): jnp.einsum('pjkab,pkbc->pjac', tiles_here, picks_here, precision=highest)  19.6 us
    reduce_scatter x1, waiting for transfers between devices, on_device(): lax.psum_scatter(hat_part, 'row', scatter_dimension=1, tiled=True)  17.8 us
  transfers between devices with their start and end apart: 7, of which 7 were waited for; matrix products, arithmetic and copies ran while one was open for 7% of the time, Pallas kernels for 0%

commit v1 on v0

--- a/solution.py
+++ b/solution.py
@@ -41,7 +41,17 @@
     owner_cols = lax.dynamic_slice_in_dim(par_struct, my_col * pair_width, pair_width, 1) - col_base
     root_row = my_col * pair_width // slot_share
     within = my_col * pair_width - root_row * slot_share
-    every_hat = lax.all_gather(par_hat, "col", axis=0, tiled=True)
+    axis_len = lax.axis_size("col")
+    found = [par_hat]
+    for hop_no in range(axis_len - 1):
+        found.append(
+            lax.ppermute(
+                found[-1], "col", [(tick, (tick + 1) % axis_len) for tick in range(axis_len)]
+            )
+        )
+    every_hat = jnp.roll(
+        jnp.concatenate(found[::-1], 0), (lax.axis_index("col") + 1) * par_hat.shape[0], 0
+    )
     picked = lax.dynamic_slice_in_dim(every_hat, within, pair_width, 1)
     picked = spread(picked, "row", root_row)
     rows_here = owner_rows

time: 443 us -> 466 us (1.052)
  waiting for transfers between devices: 342 us -> 361 us
    ppermute x0 -> x7, waiting for transfers between devices: none -> 66.8 us  [on_device(): lax.ppermute(found[-1], 'col', [(tick, (tick + 1) % axis_len) for tick in...]
    all_gather x1 -> x0, waiting for transfers between devices: 51.1 us -> none  [on_device(): every_hat = lax.all_gather(par_hat, 'col', axis=0, tiled=True)]
    unnamed x27 -> x52, local copies, waits for them, and re-layouts: 1.97 us -> 8.03 us
    psum x1, waiting for transfers between devices: 20.7 us -> 26.4 us  [spread(): return lax.psum(jnp.where(mine, array, jnp.zeros_like(array)), axis)]
    reduce_scatter x2, waiting for transfers between devices: 137 us -> 131 us  [on_device(): lax.psum_scatter(jnp.einsum('pjkab,pkbc->pjac', tiles_here, picks_here, p...]
  transfers between devices with their start and end apart: 7 -> 13, of which waited for: 7 -> 13; matrix products, arithmetic and copies ran while one was open for 7% -> 5% of each run, Pallas kernels for 0% -> 0%
where the time goes in v1:
time: 466 us; the launch traced here: 465 us
  waiting for transfers between devices  361 us (77%)
  matrix products  33.1 us (7%)
  blocking collectives  28.1 us (6%)
  local copies, waits for them, and re-layouts  20.3 us (4%)
  between operations  14.5 us (3%)
  other arithmetic  5.61 us (1%)
    reduce_scatter x2, waiting for transfers between devices, on_device(): lax.psum_scatter(jnp.einsum('pjkab,pkbc->pjac', tiles_here, picks_here, p...  131 us
    all_gather x1, waiting for transfers between devices, on_device(): every_kid = lax.all_gather(kid_hat, 'col', axis=0, tiled=True)  70.5 us
    ppermute x7, waiting for transfers between devices, on_device(): lax.ppermute(found[-1], 'col', [(tick, (tick + 1) % axis_len) for tick in...  66.8 us
    psum x1, waiting for transfers between devices, on_device(): par_diag_full = pivot_term + lax.psum(diag_part, 'row')  48.1 us
    psum x1, waiting for transfers between devices, spread(): return lax.psum(jnp.where(mine, array, jnp.zeros_like(array)), axis)  26.4 us
    dot_general x2, matrix products, on_device(): jnp.einsum('pjkab,pkbc->pjac', tiles_here, picks_here, precision=highest)  19.7 us
    reduce_scatter x1, waiting for transfers between devices, on_device(): lax.psum_scatter(hat_part, 'row', scatter_dimension=1, tiled=True)  17.8 us
  transfers between devices with their start and end apart: 13, of which 13 were waited for; matrix products, arithmetic and copies ran while one was open for 5% of the time, Pallas kernels for 0%

profile of v1, /device:TPU:0, one launch (start us, length us, event | category | flops | bytes accessed | tf_op | source)
XLA Modules:
  0.0 465.0 jit_solution(12388048182553255253)
XLA Ops:
  7.2 6.6 %all_gather.18 = f32[1,128,128]{2,1,0:T(8,128)S(1)} all-gather(f32[1,32,128]{2,1,0:T(8,128)} %param.12), channel_id=1, replica_groups=mesh['row'=4,'col'=8] {'row'}, dimensions={1}, use_global_device_ids=true | all-gather | bytes 81920 | tf_op jit(solution)/shard_map/all_gather | solution.py:36
  13.8 1.3 fusion.14
  15.1 2.0 collective-permute-start
  17.1 9.8 %collective-permute-done = f32[1,4,128,128]{3,2,1,0:T(8,128)S(1)} collective-permute-done((f32[1,4,128,128]{3,2,1,0:T(8,128)S(1)}, f32[1,4,128,128]{3,2,1,0:T(8,128)S(1)}, u32[]{:S(2)}, u32[]{:S(2)}) %collective-permute-start) | collective-permute-done | bytes 262176 | tf_op jit(solution)/shard_map/ppermute | solution.py:48
  27.0 10.8 %collective-permute-done.1 = f32[1,4,128,128]{3,2,1,0:T(8,128)S(1)} collective-permute-done((f32[1,4,128,128]{3,2,1,0:T(8,128)S(1)}, f32[1,4,128,128]{3,2,1,0:T(8,128)S(1)}, u32[]{:S(2)}, u32[]{:S(2)}) %collective-permute-start.1) | collective-permute-done | bytes 262176 | tf_op jit(solution)/shard_map/ppermute | solution.py:48
  37.7 9.9 %collective-permute-done.2 = f32[1,4,128,128]{3,2,1,0:T(8,128)S(1)} collective-permute-done((f32[1,4,128,128]{3,2,1,0:T(8,128)S(1)}, f32[1,4,128,128]{3,2,1,0:T(8,128)S(1)}, u32[]{:S(2)}, u32[]{:S(2)}) %collective-permute-start.2) | collective-permute-done | bytes 262176 | tf_op jit(solution)/shard_map/ppermute | solution.py:48
  47.6 9.1 %collective-permute-done.3 = f32[1,4,128,128]{3,2,1,0:T(8,128)S(1)} collective-permute-done((f32[1,4,128,128]{3,2,1,0:T(8,128)S(1)}, f32[1,4,128,128]{3,2,1,0:T(8,128)S(1)}, u32[]{:S(2)}, u32[]{:S(2)}) %collective-permute-start.3) | collective-permute-done | bytes 262176 | tf_op jit(solution)/shard_map/ppermute | solution.py:48
  56.7 9.1 %collective-permute-done.4 = f32[1,4,128,128]{3,2,1,0:T(8,128)S(1)} collective-permute-done((f32[1,4,128,128]{3,2,1,0:T(8,128)S(1)}, f32[1,4,128,128]{3,2,1,0:T(8,128)S(1)}, u32[]{:S(2)}, u32[]{:S(2)}) %collective-permute-start.4) | collective-permute-done | bytes 262176 | tf_op jit(solution)/shard_map/ppermute | solution.py:48
  65.8 9.1 %collective-permute-done.5 = f32[1,4,128,128]{3,2,1,0:T(8,128)S(1)} collective-permute-done((f32[1,4,128,128]{3,2,1,0:T(8,128)S(1)}, f32[1,4,128,128]{3,2,1,0:T(8,128)S(1)}, u32[]{:S(2)}, u32[]{:S(2)}) %collective-permute-start.5) | collective-permute-done | bytes 262176 | tf_op jit(solution)/shard_map/ppermute | solution.py:48
  74.9 9.1 %collective-permute-done.6 = f32[1,4,128,128]{3,2,1,0:T(8,128)S(1)} collective-permute-done((f32[1,4,128,128]{3,2,1,0:T(8,128)S(1)}, f32[1,4,128,128]{3,2,1,0:T(8,128)S(1)}, u32[]{:S(2)}, u32[]{:S(2)}) %collective-permute-start.6) | collective-permute-done | bytes 262176 | tf_op jit(solution)/shard_map/ppermute | solution.py:48
  92.3 1.7 reshape.153
  94.1 1.9 copy.51
  96.0 2.8 gather_fusion
  98.8 26.4 %all-reduce.4.cloned.1.call-done = f32[8,2,128,128]{3,2,1,0:T(8,128)} async-done(((f32[8,2,128,128]{3,2,1,0:T(8,128)}), f32[8,2,128,128]{3,2,1,0:T(8,128)}) %all-reduce.4.cloned.1.call-update) | async-done | bytes 1048592 | tf_op jit(solution)/shard_map/psum | solution.py:11
  125.2 7.5 %convolution_bitcast_fusion.1 = f32[8,4,128,128]{3,2,1,0:T(8,128)} fusion(f32[8,4,2,128,128]{4,3,2,1,0:T(8,128)} %bitcast.129, f32[8,2,128,128]{3,2,1,0:T(8,128)} %all-reduce.4.cloned.1.call-done), kind=kOutput, calls=%fused_computation.5 | convolution fusion | flops 1610612736 | bytes 7340032 | tf_op jit(solution)/shard_map/pjkab,pkbc->pjac/dot_general | solution.py:62
  132.9 5.4 %all_gather.20 = f32[2,128,128]{2,1,0:T(8,128)S(1)} all-gather(f32[2,32,128]{2,1,0:T(8,128)S(1)} %copy-done.13), channel_id=1, replica_groups=mesh['row'=4,'col'=8] {'row'}, dimensions={1}, use_global_device_ids=true | all-gather | bytes 163840 | tf_op jit(solution)/shard_map/all_gather | solution.py:76
  138.3 1.4 fusion.17
  139.8 61.1 %reduce-scatter.4.cloned.1.call-done = f32[1,4,128,128]{3,2,1,0:T(8,128)} async-done(((f32[8,4,128,128]{3,2,1,0:T(8,128)}), f32[1,4,128,128]{3,2,1,0:T(8,128)}) %reduce-scatter.4.cloned.1.call-update) | async-done | bytes 262160 | tf_op jit(solution)/shard_map/reduce_scatter | solution.py:61
  201.9 1.2 fusion.8
  203.1 2.7 convolution_bitcast_fusion.4
  205.8 70.5 %all-gather.2.cloned.1.call-done = f32[16,4,128,128]{3,2,1,0:T(8,128)} async-done(((f32[2,4,128,128]{3,2,1,0:T(8,128)}), f32[16,4,128,128]{3,2,1,0:T(8,128)}) %all-gather.2.cloned.1.call-update) | async-done | bytes 4194320 | tf_op jit(solution)/shard_map/all_gather | solution.py:83
  276.3 3.2 dynamic-slice_select_fusion
  280.3 4.5 gather_fusion.1
  284.8 48.1 %all-reduce.6.cloned.1.call-done = (f32[1,128,128]{2,1,0:T(8,128)}, f32[16,2,128,128]{3,2,1,0:T(8,128)}, f32[2,128,128]{1,2,0:T(8,128)}) async-done(((f32[1,128,128]{2,1,0:T(8,128)}, f32[16,2,128,128]{3,2,1,0:T(8,128)}, f32[2,128,128]{1,2,0:T(8,128)}), (f32[1,128,128]{2,1,0:T(8,128)}, f32[16,2,128,128]{3,2,1,0:T(8,128)}, f32[2,128,128]{1,2,0:T(8,128)})) %all-reduce.6.cloned.1.call-update) | async-done | bytes 2293776 | tf_op jit(solution)/shard_map/psum | solution.py:72
  332.9 12.1 %convolution_bitcast_fusion = f32[16,4,128,128]{3,2,1,0:T(8,128)} fusion(f32[16,4,2,128,128]{4,3,2,1,0:T(8,128)} %bitcast.128, f32[16,2,128,128]{3,2,1,0:T(8,128)} %get-tuple-element.26), kind=kOutput, calls=%fused_computation.2 | convolution fusion | flops 3221225472 | bytes 14680064 | tf_op jit(solution)/shard_map/pjkab,pkbc->pjac/dot_general | solution.py:91
  345.7 5.2 %all_gather.19 = f32[1,128,128]{2,1,0:T(8,128)S(1)} all-gather(f32[1,32,128]{2,1,0:T(8,128)S(1)} %copy-done.16), channel_id=1, replica_groups=mesh['row'=4,'col'=8] {'row'}, dimensions={1}, use_global_device_ids=true | all-gather | bytes 81920 | tf_op jit(solution)/shard_map/all_gather | solution.py:37
  351.0 5.4 %all_gather.22 = f32[2,128,128]{2,1,0:T(8,128)S(1)} all-gather(f32[2,32,128]{2,1,0:T(8,128)S(1)} %copy-done.14), channel_id=1, replica_groups=mesh['row'=4,'col'=8] {'row'}, dimensions={1}, use_global_device_ids=true | all-gather | bytes 163840 | tf_op jit(solution)/shard_map/all_gather | solution.py:75
  356.4 5.4 %all_gather.23 = f32[2,128,128]{2,1,0:T(8,128)S(1)} all-gather(f32[2,32,128]{2,1,0:T(8,128)S(1)} %copy-done.15), channel_id=1, replica_groups=mesh['row'=4,'col'=8] {'row'}, dimensions={1}, use_global_device_ids=true | all-gather | bytes 163840 | tf_op jit(solution)/shard_map/all_gather | solution.py:77
  363.2 70.2 %reduce-scatter.6.cloned.1.call-done = f32[2,4,128,128]{3,2,1,0:T(8,128)} async-done(((f32[16,4,128,128]{3,2,1,0:T(8,128)}), f32[2,4,128,128]{3,2,1,0:T(8,128)}) %reduce-scatter.6.cloned.1.call-update) | async-done | bytes 524304 | tf_op jit(solution)/shard_map/reduce_scatter | solution.py:90
  433.4 1.6 fusion.3
  435.0 1.7 fusion.4
  438.4 17.8 %reduce-scatter.8.cloned.1.call-done = f32[2,32,128]{2,1,0:T(8,128)} async-done(((f32[2,128,128]{2,1,0:T(8,128)}), f32[2,32,128]{2,1,0:T(8,128)}) %reduce-scatter.8.cloned.1.call-update) | async-done | bytes 32784 | tf_op jit(solution)/shard_map/reduce_scatter | solution.py:119
  (95 shorter events, 15.9 us)
Async XLA Ops:
  7.2 131.1 %copy-start = (f32[2,4,128,128]{3,2,1,0:T(8,128)S(1)}, f32[2,4,128,128]{3,2,1,0:T(8,128)}, u32[]{:S(2)}) copy-start(f32[2,4,128,128]{3,2,1,0:T(8,128)} %param.14) | copy-start | bytes 1572868
  7.2 118.1 %all-reduce.4.cloned.1.call-start = ((), (), s32[]{:S(2)}) async-start(), calls=%async_computation.3 | async-start | bytes 2097152 | tf_op jit(solution)/shard_map/psum | solution.py:11
  15.1 11.8 %collective-permute-start = (f32[1,4,128,128]{3,2,1,0:T(8,128)S(1)}, f32[1,4,128,128]{3,2,1,0:T(8,128)S(1)}, u32[]{:S(2)}, u32[]{:S(2)}) collective-permute-start(f32[1,4,128,128]{3,2,1,0:T(8,128)S(1)} %bitcast.130), channel_id=1, source_target_pairs={{0,1},{1,2},{2,3},{3,4},{4,5},{5,6},{6,7},{7,0},{8,9},{9,10},{10,1... | collective-permute-start | bytes 786440 | tf_op jit(solution)/shard_map/ppermute | solution.py:48
  27.0 10.8 %collective-permute-start.1 = (f32[1,4,128,128]{3,2,1,0:T(8,128)S(1)}, f32[1,4,128,128]{3,2,1,0:T(8,128)S(1)}, u32[]{:S(2)}, u32[]{:S(2)}) collective-permute-start(f32[1,4,128,128]{3,2,1,0:T(8,128)S(1)} %collective-permute-done), channel_id=1, source_target_pairs={{0,1},{1,2},{2,3},{3,4},{4,5},{5,6},{6,7},{7,0},{8,9},{9,10},{10,1... | collective-permute-start | bytes 786440 | tf_op jit(solution)/shard_map/ppermute | solution.py:48
  37.7 46.3 %copy-start.5 = (f32[1,4,128,128]{3,2,1,0:T(8,128)}, f32[1,4,128,128]{3,2,1,0:T(8,128)S(1)}, u32[]{:S(2)}) copy-start(f32[1,4,128,128]{3,2,1,0:T(8,128)S(1)} %collective-permute-done.1) | copy-start | bytes 786436
  37.7 9.9 %collective-permute-start.2 = (f32[1,4,128,128]{3,2,1,0:T(8,128)S(1)}, f32[1,4,128,128]{3,2,1,0:T(8,128)S(1)}, u32[]{:S(2)}, u32[]{:S(2)}) collective-permute-start(f32[1,4,128,128]{3,2,1,0:T(8,128)S(1)} %collective-permute-done.1), channel_id=1, source_target_pairs={{0,1},{1,2},{2,3},{3,4},{4,5},{5,6},{6,7},{7,0},{8,9},{9,10},{10,1... | collective-permute-start | bytes 786440 | tf_op jit(solution)/shard_map/ppermute | solution.py:48
  47.6 36.5 %copy-start.6 = (f32[1,4,128,128]{3,2,1,0:T(8,128)}, f32[1,4,128,128]{3,2,1,0:T(8,128)S(1)}, u32[]{:S(2)}) copy-start(f32[1,4,128,128]{3,2,1,0:T(8,128)S(1)} %collective-permute-done.2) | copy-start | bytes 786436
  47.6 9.1 %collective-permute-start.3 = (f32[1,4,128,128]{3,2,1,0:T(8,128)S(1)}, f32[1,4,128,128]{3,2,1,0:T(8,128)S(1)}, u32[]{:S(2)}, u32[]{:S(2)}) collective-permute-start(f32[1,4,128,128]{3,2,1,0:T(8,128)S(1)} %collective-permute-done.2), channel_id=1, source_target_pairs={{0,1},{1,2},{2,3},{3,4},{4,5},{5,6},{6,7},{7,0},{8,9},{9,10},{10,1... | collective-permute-start | bytes 786440 | tf_op jit(solution)/shard_map/ppermute | solution.py:48
  56.7 27.4 %copy-start.7 = (f32[1,4,128,128]{3,2,1,0:T(8,128)}, f32[1,4,128,128]{3,2,1,0:T(8,128)S(1)}, u32[]{:S(2)}) copy-start(f32[1,4,128,128]{3,2,1,0:T(8,128)S(1)} %collective-permute-done.3) | copy-start | bytes 786436
  56.7 9.1 %collective-permute-start.4 = (f32[1,4,128,128]{3,2,1,0:T(8,128)S(1)}, f32[1,4,128,128]{3,2,1,0:T(8,128)S(1)}, u32[]{:S(2)}, u32[]{:S(2)}) collective-permute-start(f32[1,4,128,128]{3,2,1,0:T(8,128)S(1)} %collective-permute-done.3), channel_id=1, source_target_pairs={{0,1},{1,2},{2,3},{3,4},{4,5},{5,6},{6,7},{7,0},{8,9},{9,10},{10,1... | collective-permute-start | bytes 786440 | tf_op jit(solution)/shard_map/ppermute | solution.py:48
  65.8 18.3 %copy-start.8 = (f32[1,4,128,128]{3,2,1,0:T(8,128)}, f32[1,4,128,128]{3,2,1,0:T(8,128)S(1)}, u32[]{:S(2)}) copy-start(f32[1,4,128,128]{3,2,1,0:T(8,128)S(1)} %collective-permute-done.4) | copy-start | bytes 786436
  65.8 9.1 %collective-permute-start.5 = (f32[1,4,128,128]{3,2,1,0:T(8,128)S(1)}, f32[1,4,128,128]{3,2,1,0:T(8,128)S(1)}, u32[]{:S(2)}, u32[]{:S(2)}) collective-permute-start(f32[1,4,128,128]{3,2,1,0:T(8,128)S(1)} %collective-permute-done.4), channel_id=1, source_target_pairs={{0,1},{1,2},{2,3},{3,4},{4,5},{5,6},{6,7},{7,0},{8,9},{9,10},{10,1... | collective-permute-start | bytes 786440 | tf_op jit(solution)/shard_map/ppermute | solution.py:48
  74.9 9.2 %copy-start.9 = (f32[1,4,128,128]{3,2,1,0:T(8,128)}, f32[1,4,128,128]{3,2,1,0:T(8,128)S(1)}, u32[]{:S(2)}) copy-start(f32[1,4,128,128]{3,2,1,0:T(8,128)S(1)} %collective-permute-done.5) | copy-start | bytes 786436
  74.9 9.1 %collective-permute-start.6 = (f32[1,4,128,128]{3,2,1,0:T(8,128)S(1)}, f32[1,4,128,128]{3,2,1,0:T(8,128)S(1)}, u32[]{:S(2)}, u32[]{:S(2)}) collective-permute-start(f32[1,4,128,128]{3,2,1,0:T(8,128)S(1)} %collective-permute-done.5), channel_id=1, source_target_pairs={{0,1},{1,2},{2,3},{3,4},{4,5},{5,6},{6,7},{7,0},{8,9},{9,10},{10,1... | collective-permute-start | bytes 786440 | tf_op jit(solution)/shard_map/ppermute | solution.py:48
  83.9 0.7 copy-start.10
  84.7 7.3 %copy-start.17 = (s32[8,16]{1,0:T(8,128)S(1)}, s32[8,16]{1,0:T(8,128)}, u32[]{:S(2)}) copy-start(s32[8,16]{1,0:T(8,128)} %param.10) | copy-start | bytes 1540
  84.7 7.7 %copy-start.3 = (f32[1024,512]{1,0:T(8,128)S(1)}, f32[1024,512]{1,0:T(8,128)}, u32[]{:S(2)}) copy-start(f32[1024,512]{1,0:T(8,128)} %param.9) | copy-start | bytes 6291460
  91.9 109.0 %reduce-scatter.4.cloned.1.call-start = ((), (), s32[]{:S(2)}) async-start(), calls=%async_computation.4 | async-start | bytes 2359296 | tf_op jit(solution)/shard_map/reduce_scatter | solution.py:61
  125.2 7.6 %copy-start.13 = (f32[2,32,128]{2,1,0:T(8,128)S(1)}, f32[2,32,128]{2,1,0:T(8,128)}, u32[]{:S(2)}) copy-start(f32[2,32,128]{2,1,0:T(8,128)} %param.16) | copy-start | bytes 98308
  132.8 143.4 %all-gather.2.cloned.1.call-start = ((), (), s32[]{:S(2)}) async-start(), calls=%async_computation.5 | async-start | bytes 4718592 | tf_op jit(solution)/shard_map/all_gather | solution.py:83
  139.7 193.2 %all-reduce.6.cloned.1.call-start = ((), (), s32[]{:S(2)}) async-start(), calls=%async_computation.8 | async-start | bytes 4587520 | tf_op jit(solution)/shard_map/psum | solution.py:72
  201.9 231.5 %copy-start.2 = (f32[1,4,128,128]{3,2,1,0:T(8,128)}, f32[1,4,128,128]{3,2,1,0:T(8,128)S(1)}, u32[]{:S(2)}) copy-start(f32[1,4,128,128]{3,2,1,0:T(8,128)S(1)} %neg.18) | copy-start | bytes 786436
  279.5 153.9 %reduce-scatter.6.cloned.1.call-start = ((), (), s32[]{:S(2)}) async-start(), calls=%async_computation.6 | async-start | bytes 4718592 | tf_op jit(solution)/shard_map/reduce_scatter | solution.py:90
  345.0 0.7 copy-start.16
  345.0 5.9 %copy-start.14 = (f32[2,32,128]{2,1,0:T(8,128)S(1)}, f32[2,32,128]{2,1,0:T(8,128)}, u32[]{:S(2)}) copy-start(f32[2,32,128]{2,1,0:T(8,128)} %param.15) | copy-start | bytes 98308
  345.0 11.4 %copy-start.15 = (f32[2,32,128]{2,1,0:T(8,128)S(1)}, f32[2,32,128]{2,1,0:T(8,128)}, u32[]{:S(2)}) copy-start(f32[2,32,128]{2,1,0:T(8,128)} %param.17) | copy-start | bytes 98308
  345.0 17.9 %copy-start.12 = (f32[1,128,128]{2,1,0:T(8,128)S(1)}, f32[1,128,128]{2,1,0:T(8,128)}, u32[]{:S(2)}) copy-start(f32[1,128,128]{2,1,0:T(8,128)} %get-tuple-element.25) | copy-start | bytes 196612
  345.0 90.0 %copy-start.1 = (f32[2,4,128,128]{3,2,1,0:T(8,128)S(1)}, f32[2,4,128,128]{3,2,1,0:T(8,128)}, u32[]{:S(2)}) copy-start(f32[2,4,128,128]{3,2,1,0:T(8,128)} %fusion.17) | copy-start | bytes 1572868
  345.0 91.7 %copy-start.11 = (f32[2,128,128]{1,2,0:T(8,128)S(1)}, f32[2,128,128]{1,2,0:T(8,128)}, u32[]{:S(2)}) copy-start(f32[2,128,128]{1,2,0:T(8,128)} %get-tuple-element.27) | copy-start | bytes 393220
  345.1 111.2 %reduce-scatter.8.cloned.1.call-start = ((), (), s32[]{:S(2)}) async-start(), calls=%async_computation.7 | async-start | bytes 163840 | tf_op jit(solution)/shard_map/reduce_scatter | solution.py:119
  435.0 23.1 %copy-start.4 = (f32[2,4,128,128]{3,2,1,0:T(8,128)}, f32[2,4,128,128]{3,2,1,0:T(8,128)S(1)}, u32[]{:S(2)}) copy-start(f32[2,4,128,128]{3,2,1,0:T(8,128)S(1)} %fusion.3) | copy-start | bytes 1572868
Sparse Core Ops, SparseCore 0:
  92.0 33.1 all-reduce.3
  132.9 67.9 reduce-scatter.3
  203.8 72.3 all-gather.1
  279.6 53.2 all-reduce.5
  345.2 88.1 reduce-scatter.5
  436.8 19.3 reduce-scatter.7
